TPU v7x, 32 devices: a whole 2x2x4 slice. The times are simulated.
32 devices in a mesh: dp: 8 (over z, core), seq: 4 (over y, x).
Axes of the slice: x: 2, y: 2, z: 4, core: 2. Of those that a mesh axis runs over, the one named last changes fastest.
Arguments:
- waveform: bfloat16 [32, 2560], P('dp', 'seq'), may hold values from -6 to 6
- lengths: int32 [8, 4], P('dp'), may hold values from 1 to 2560, 6400 in all within a row
- conv_one: bfloat16 [10, 512], replicated, may hold values from -2 to 2
- conv_two: bfloat16 [1536, 512], replicated, may hold values from -0.15625 to 0.15625
- gain_one: float32 [512], replicated, may hold values from 0.1 to 1.9
- shift_one: float32 [512], replicated, may hold values from -3 to 3
- gain_two: float32 [512], replicated, may hold values from 0.1 to 1.9
- shift_two: float32 [512], replicated, may hold values from -3 to 3
- cotangent: bfloat16 [32, 256, 512], P('dp', 'seq'), may hold values from -0.0625 to 0.0625
Outputs:
- features: bfloat16 [32, 256, 512], P('dp', 'seq')
- conv_one_grad: float32 [10, 512], replicated
- conv_two_grad: float32 [1536, 512], P('seq')
- norm_grads: float32 [4, 512], replicated
Inputs may be any that keep to these rules, and one draw needn't show every extreme that they name: In each row of lengths the 4 lengths sum to 6400 and the longest is exactly 2560.
All inputs are finite; a program needn't handle non-finite values.
Results may differ from a plain program's by a relative error of at most 0.0054.
Values may be sent and summed in bfloat16 or wider, within the bound.
A program may use at most 64 MiB of HBM per device.

v0:
```python
import jax
import jax.numpy as jnp
from jax import lax
from jax.sharding import PartitionSpec as P

epsilon = 1e-05
root_half = 0.7071067811865476
normal_peak = 0.3989422804014327


def passed_along(value, axis, steps):
    count = lax.axis_size(axis)
    first, last = (max(0, -steps), min(count, count - steps))
    return lax.ppermute(value, axis, [(source, source + steps) for source in range(first, last)])


def norm_forward(preact, gain_vector, offset):
    centre = preact - jnp.mean(preact, axis=-1, keepdims=True)
    inverse = lax.rsqrt(jnp.mean(centre * centre, axis=-1, keepdims=True) + epsilon)
    normed = centre * inverse
    return (normed, inverse, normed * gain_vector + offset)


def gelu_slope(values):
    return (
        0.5 * (1.0 + lax.erf(values * root_half))
        + values * jnp.exp(-0.5 * values * values) * normal_peak
    )


def norm_backward(upstream, normed, inverse, gain_vector):
    scaled = upstream * gain_vector
    return inverse * (
        scaled
        - jnp.mean(scaled, axis=-1, keepdims=True)
        - normed * jnp.mean(scaled * normed, axis=-1, keepdims=True)
    )


def on_device(
    waveform, lengths, conv_one, conv_two, gain_one, shift_one, gain_two, shift_two, cotangent
):
    clip_count, samples = waveform.shape
    frames_one = samples // 5
    frames_two = cotangent.shape[1]
    channels = conv_two.shape[1]
    position = lax.axis_index("seq")
    border = passed_along(waveform[:, :16], "seq", -1)
    extended = jnp.concatenate([waveform, border], axis=1)
    blocks = extended[:, : 5 * (frames_one + 1)].reshape(clip_count, frames_one + 1, 5)
    patch_one = jnp.concatenate([blocks[:, :-1], blocks[:, 1:]], axis=2).reshape(
        clip_count * frames_one, 10
    )
    pre_one = jnp.dot(patch_one, conv_one, preferred_element_type=jnp.float32)
    normed_one, inverse_one, output_one = norm_forward(pre_one, gain_one, shift_one)
    active_one = (
        jax.nn.gelu(output_one, approximate=False)
        .astype(jnp.bfloat16)
        .reshape(clip_count, frames_one, channels)
    )
    edge_frame = passed_along(active_one[:, :1], "seq", -1)
    widened = jnp.concatenate([active_one, edge_frame], axis=1)
    patch_two = jnp.concatenate(
        [widened[:, :frames_one].reshape(clip_count, frames_two, 2 * channels), widened[:, 2::2]],
        axis=2,
    ).reshape(clip_count * frames_two, 3 * channels)
    pre_two = jnp.dot(patch_two, conv_two, preferred_element_type=jnp.float32)
    normed_two, inverse_two, output_two = norm_forward(pre_two, gain_two, shift_two)
    lengths_row = lengths[0]
    first_frames = (lengths_row - 5) // 5
    second_frames = (first_frames - 1) // 2
    frame_index = position * frames_two + lax.broadcasted_iota(
        jnp.int32, (clip_count, frames_two), 1
    )
    validity = (
        (frame_index < second_frames[:, None])
        .astype(jnp.float32)
        .reshape(clip_count * frames_two, 1)
    )
    features = (
        (jax.nn.gelu(output_two, approximate=False) * validity)
        .astype(jnp.bfloat16)
        .reshape(clip_count, frames_two, channels)
    )
    upstream_two = (
        cotangent.reshape(clip_count * frames_two, channels).astype(jnp.float32)
        * validity
        * gelu_slope(output_two)
    )
    dpre_two = norm_backward(upstream_two, normed_two, inverse_two, gain_two).astype(jnp.bfloat16)
    dpatch_two = lax.dot_general(
        dpre_two, conv_two, (((1,), (1,)), ((), ())), preferred_element_type=jnp.float32
    ).reshape(clip_count, frames_two, 3 * channels)
    paired = dpatch_two[:, :, : 2 * channels].reshape(clip_count, frames_two, 2, channels)
    onward = dpatch_two[:, :, 2 * channels :]
    carried = jnp.concatenate([passed_along(onward[:, -1:], "seq", 1), onward[:, :-1]], axis=1)
    dact_one = jnp.stack([paired[:, :, 0] + carried, paired[:, :, 1]], axis=2).reshape(
        clip_count, frames_one, channels
    )
    upstream_one = dact_one.reshape(clip_count * frames_one, channels) * gelu_slope(output_one)
    dpre_one = norm_backward(upstream_one, normed_one, inverse_one, gain_one)
    grad_one = lax.dot_general(
        patch_one.astype(jnp.float32),
        dpre_one,
        (((0,), (0,)), ((), ())),
        precision=lax.Precision.HIGHEST,
        preferred_element_type=jnp.float32,
    )
    norm_terms = jnp.stack(
        [
            jnp.sum(upstream_one * normed_one, 0),
            jnp.sum(upstream_one, 0),
            jnp.sum(upstream_two * normed_two, 0),
            jnp.sum(upstream_two, 0),
        ]
    )
    grad_one_sum, norm_sum = lax.psum((grad_one, norm_terms), ("dp", "seq"))
    seq_share = lax.psum_scatter(
        lax.dot_general(
            patch_two, dpre_two, (((0,), (0,)), ((), ())), preferred_element_type=jnp.float32
        ),
        "seq",
        scatter_dimension=0,
        tiled=True,
    )
    grad_two = lax.psum(seq_share, "dp")
    return (features, grad_one_sum, grad_two, norm_sum)


def solution(mesh):
    in_specs = (P("dp", "seq"), P("dp", None), P(), P(), P(), P(), P(), P(), P("dp", "seq", None))
    out_specs = (P("dp", "seq", None), P(), P("seq", None), P())
    return jax.shard_map(
        on_device, mesh=mesh, in_specs=in_specs, out_specs=out_specs, check_vma=False
    )
```

profile of v0, /device:TPU:0, one launch (start us, length us, event | category | flops | bytes accessed | tf_op | source)
XLA Modules:
  0.0 152.2 jit_solution(17305733421126608220)
XLA Ops:
  7.2 0.0 copy-start
  7.2 0.0 reduce-scatter.2.cloned.1.call-start
  7.2 0.8 slice.36
  8.0 1.3 collective-permute-start
  9.3 0.7 and_select_fusion
  10.0 4.4 %collective-permute-done = bf16[4,16]{1,0:T(4,128)(2,1)S(1)} collective-permute-done((bf16[4,16]{1,0:T(4,128)(2,1)S(1)}, bf16[4,16]{1,0:T(4,128)(2,1)S(1)}, u32[]{:S(2)}, u32[]{:S(2)}) %collective-permute-start) | collective-permute-done | bytes 160 | tf_op jit(solution)/shard_map/ppermute | solution.py:14
  14.4 0.7 pad_maximum_fusion.6
  15.1 0.0 copy-start.5
  15.1 0.0 copy-start.6
  15.1 0.2 reshape.138
  15.4 0.1 copy.16
  15.5 0.1 copy.17
  15.7 1.1 fusion.49
  16.8 0.3 multiply_reduce_fusion.2
  17.1 0.0 copy-done.5
  17.1 0.0 copy-done.6
  17.1 3.0 %fusion.2 = bf16[512,512]{1,0:T(8,128)(2,1)S(1)} fusion(f32[512,512]{1,0:T(8,128)S(1)} %get-tuple-element.22, f32[512]{0:T(512)S(1)} %copy-done.6, f32[512]{0:T(512)S(1)} %copy-done.5, f32[512]{0:T(512)S(1)} %add_rsqrt_fusion, f32[512]{0:T(512)S(1)} %broadcast_multiply_fusion.2), kind=kLoop, calls=%fused_computation.4 | loop fusion | flops 18087936 | bytes 1581056 | tf_op jit(solution)/shard_map/convert_element_type | solution.py:58
  20.1 1.3 collective-permute-start.1
  21.4 0.1 compare_convert_fusion
  21.5 0.1 reshape.144
  21.6 1.0 concatenate.27
  22.6 4.0 %collective-permute-done.1 = bf16[4,1,512]{2,1,0:T(2,128)(2,1)S(1)} collective-permute-done((bf16[4,1,512]{2,1,0:T(2,128)(2,1)S(1)}, bf16[4,1,512]{2,1,0:T(2,128)(2,1)S(1)}, u32[]{:S(2)}, u32[]{:S(2)}) %collective-permute-start.1) | collective-permute-done | bytes 4128 | tf_op jit(solution)/shard_map/ppermute | solution.py:14
  26.6 0.9 pad_maximum_fusion.2
  27.4 2.1 %slice.41 = bf16[4,64,512]{2,1,0:T(8,128)(2,1)S(1)} slice(bf16[4,129,512]{2,1,0:T(8,128)(2,1)} %pad_maximum_fusion.2), slice={[0:4:1], [2:129:2], [0:512:1]} | slice | bytes 524288 | tf_op jit(solution)/shard_map/slice | solution.py:64
  29.5 0.0 copy-done
  29.6 0.0 copy-start.3
  29.6 0.0 copy-start.4
  29.6 0.0 copy-start.7
  29.6 1.7 %fusion.50 = (f32[256]{0:T(256)S(1)}, f32[256,512]{1,0:T(8,128)S(1)}) fusion(bf16[1536,512]{1,0:T(8,128)(2,1)S(1)} %copy-done, bf16[256,512]{1,0:T(8,128)(2,1)S(1)} %bitcast.39, bf16[256,1024]{1,0:T(8,128)(2,1)} %concatenate.27), kind=kOutput, calls=%fused_computation.105 | convolution fusion | flops 404356864 | bytes 2884608 | tf_op jit(solution)/shard_map/dot_general | solution.py:67
  31.3 0.0 copy-start.2
  31.3 0.2 multiply_reduce_fusion.6
  31.6 0.0 copy-done.3
  31.6 0.0 copy-done.4
  31.6 0.0 copy-done.7
  31.6 2.5 %multiply_reduce_fusion.4 = (f32[512]{0:T(512)S(1)}, f32[256]{0:T(256)S(1)}, f32[256]{0:T(256)S(1)}, f32[512]{0:T(512)S(1)}, f32[256,512]{1,0:T(8,128)S(1)}, /*index=5*/bf16[256,512]{1,0:T(8,128)(2,1)}) fusion(f32[256,512]{1,0:T(8,128)S(1)} %get-tuple-element.24, f32[256]{0:T(256)S(1)} %add_rsqrt_fusion.1, f32[256]{0:T(256)S(1)} %broadcast_multiply_fusion.5, ...), kind=kLoop, calls=%fused_computation.54 | loop fusion | flops 11532800 | bytes 1586176 | tf_op jit(solution)/shard_map/reduce_sum | solution.py:113
  34.1 0.0 copy-start.1
  34.1 0.8 copy-done.1
  34.9 0.0 copy-done.2
  34.9 2.4 %fusion.42 = f32[1536,512]{1,0:T(8,128)} fusion(bf16[256,512]{1,0:T(8,128)(2,1)S(1)} %bitcast.40, bf16[256,1024]{1,0:T(8,128)(2,1)S(1)} %copy-done.2, f32[256,512]{1,0:T(8,128)S(1)} %get-tuple-element.15, f32[256,512]{1,0:T(8,128)S(1)} %get-tuple-element.24, f32[256]{0:T(256)S(1)} %get-tuple-element.25, f32[256]{0:T(256)S(1)} %get-tuple-element.26, ...), kind=kOutput, calls=%fused_computation.79 | convolution fusion | flops 405274624 | bytes 4986880 | tf_op jit(solution)/shard_map/dot_general | solution.py:119
  37.3 0.0 reduce-scatter.2.cloned.1.call-update
  37.4 0.0 all-reduce.3.cloned.1.call-start
  37.4 1.7 %fusion.51 = f32[256,1536]{1,0:T(8,128)S(1)} fusion(bf16[1536,512]{1,0:T(8,128)(2,1)S(1)} %copy-done, f32[256,512]{1,0:T(8,128)} %copy-done.1, f32[256,512]{1,0:T(8,128)S(1)} %get-tuple-element.24, f32[256]{0:T(256)S(1)} %get-tuple-element.25, f32[256]{0:T(256)S(1)} %get-tuple-element.26, f32[512]{0:T(512)S(1)} %copy-done.4, f32[256]{0:T(256)S(1)} %add_rsqrt_fusion.1, ...), kind=kOutput, calls=%fused_computation.106 | convolution fusion | flops 403701760 | bytes 4200448 | tf_op jit(solution)/shard_map/dot_general | solution.py:91
  39.2 5.0 %collective-permute-start.2 = (f32[4,1,512]{2,1,0:T(1,128)S(1)}, f32[4,1,512]{2,1,0:T(1,128)S(1)}, u32[]{:S(2)}, u32[]{:S(2)}) collective-permute-start(f32[4,1,512]{2,1,0:T(1,128)S(1)} %slice.52), channel_id=1, source_target_pairs={{0,1},{1,2},{2,3},{4,5},{5,6},{6,7},{8,9},{9,10},{10,11},{12,13},{... | collective-permute-start | bytes 24584 | tf_op jit(solution)/shard_map/ppermute | solution.py:14
  44.2 1.1 slice.50
  45.3 3.3 %reshape.143 = f32[4,64,2,512]{3,2,1,0:T(2,128)} reshape(f32[4,64,1024]{2,1,0:T(8,128)} %slice.50) | data formatting | bytes 2097152 | tf_op jit(solution)/shard_map/reshape | solution.py:94
  48.6 0.5 copy.18
  49.1 0.0 collective-permute-done.2
  49.1 2.8 %slice_add_fusion = (f32[4,64,1,512]{3,2,1,0:T(1,128)S(1)}, f32[4,64,1,512]{3,2,1,0:T(1,128)S(1)}) fusion(f32[4,64,2,512]{3,2,1,0:T(2,128)} %reshape.143, f32[4,63,1,512]{3,2,1,0:T(1,128)S(1)} %copy.18, f32[4,1,1,512]{3,2,1,0:T(1,128)S(1)} %bitcast.45), kind=kLoop, calls=%fused_computation.52 | loop fusion | flops 262144 | bytes 2621440 | tf_op jit(solution)/shard_map/add | solution.py:97
  52.0 1.9 %pad_maximum_fusion = f32[4,64,2,512]{3,2,1,0:T(2,128)} fusion(f32[4,64,1,512]{3,2,1,0:T(1,128)S(1)} %get-tuple-element.17, f32[4,64,1,512]{3,2,1,0:T(1,128)S(1)} %get-tuple-element.16), kind=kLoop, calls=%fused_computation.10 | loop fusion | flops 262144 | bytes 2097152 | tf_op jit(solution)/shard_map/stack | solution.py:97
  53.9 2.9 %reshape_reshape.4 = f32[512,512]{1,0:T(8,128)} reshape(f32[4,64,2,512]{3,2,1,0:T(2,128)} %pad_maximum_fusion) | data formatting | bytes 2097152 | tf_op jit(solution)/shard_map/reshape;reshape | solution.py:100
  56.8 3.0 %multiply_reduce_fusion = (f32[512]{0:T(512)S(1)}, f32[512]{0:T(512)S(1)}, f32[512]{0:T(512)S(1)}, f32[512]{0:T(512)S(1)}, f32[512,512]{1,0:T(8,128)}) fusion(f32[512,512]{1,0:T(8,128)S(1)} %get-tuple-element.22, f32[512]{0:T(512)S(1)} %add_rsqrt_fusion, f32[512]{0:T(512)S(1)} %broadcast_multiply_fusion.2, f32[512]{0:T(512)S(1)} %copy-done.5, ...), kind=kLoop, calls=%fused_computation.11 | loop fusion | flops 5240832 | bytes 3162112 | tf_op jit(solution)/shard_map/reduce_sum | solution.py:111
  59.9 23.3 %reduce-scatter.2.cloned.1.call-done = f32[384,512]{1,0:T(8,128)} async-done(((f32[1536,512]{1,0:T(8,128)}), f32[384,512]{1,0:T(8,128)}) %reduce-scatter.2.cloned.1.call-update) | async-done | bytes 786448 | tf_op jit(solution)/shard_map/reduce_scatter | solution.py:118
  83.1 0.0 all-reduce.3.cloned.1.call-update
  83.2 2.0 %fusion.8 = f32[10,512]{1,0:T(8,128)S(1)} fusion(bf16[512,10]{0,1:T(8,128)(2,1)S(1)} %bitcast.43, f32[512,512]{1,0:T(8,128)} %get-tuple-element.14, f32[512,512]{1,0:T(8,128)S(1)} %get-tuple-element.22, f32[512]{0:T(512)S(1)} %broadcast_multiply_fusion, f32[512]{0:T(512)S(1)} %broadcast_multiply_fusion.1, f32[512]{0:T(512)S(1)} %copy-done.5, ...), kind=kOutput, calls=%fused_computation.12 | convolution fusion | flops 33292288 | bytes 2138112 | tf_op jit(solution)/shard_map/dot_general | solution.py:102
  85.2 40.2 %all-reduce = (f32[10,512]{1,0:T(8,128)}, f32[4,512]{1,0:T(4,128)}) all-reduce(f32[10,512]{1,0:T(8,128)S(1)} %fusion.8, f32[4,512]{1,0:T(4,128)S(1)} %pad_maximum_fusion.5), channel_id=1, replica_groups=mesh['dp'=8,'seq'=4] {'dp','seq'}, use_global_device_ids=true, to_apply=%region_8.9 | all-reduce | flops 7168 | bytes 57344 | tf_op jit(solution)/shard_map/psum | solution.py:117
  125.4 17.9 %all-reduce.3.cloned.1.call-done = f32[384,512]{1,0:T(8,128)} async-done(((f32[384,512]{1,0:T(8,128)}), f32[384,512]{1,0:T(8,128)}) %all-reduce.3.cloned.1.call-update) | async-done | bytes 786448 | tf_op jit(solution)/shard_map/psum | solution.py:126
  143.3 2.1 %copy.21 = f32[384,512]{1,0:T(8,128)} copy(f32[384,512]{1,0:T(8,128)} %all-reduce.3.cloned.1.call-done) | data formatting | bytes 1572864
  (16 shorter events, 0.2 us)
Async XLA Ops:
  7.2 22.4 %copy-start = (bf16[1536,512]{1,0:T(8,128)(2,1)S(1)}, bf16[1536,512]{1,0:T(8,128)(2,1)}, u32[]{:S(2)}) copy-start(bf16[1536,512]{1,0:T(8,128)(2,1)} %param.12) | copy-start | bytes 4718596
  7.2 76.0 %reduce-scatter.2.cloned.1.call-start = ((), (), s32[]{:S(2)}) async-start(), calls=%async_computation.1 | async-start | bytes 3932160 | tf_op jit(solution)/shard_map/reduce_scatter | solution.py:118
  8.0 6.4 %collective-permute-start = (bf16[4,16]{1,0:T(4,128)(2,1)S(1)}, bf16[4,16]{1,0:T(4,128)(2,1)S(1)}, u32[]{:S(2)}, u32[]{:S(2)}) collective-permute-start(bf16[4,16]{1,0:T(4,128)(2,1)S(1)} %slice.36), channel_id=1, source_target_pairs={{1,0},{2,1},{3,2},{5,4},{6,5},{7,6},{9,8},{10,9},{11,10},{13,12},{... | collective-permute-start | bytes 392 | tf_op jit(solution)/shard_map/ppermute | solution.py:14
  15.1 2.0 %copy-start.5 = (f32[512]{0:T(512)S(1)}, f32[512]{0:T(512)}, u32[]{:S(2)}) copy-start(f32[512]{0:T(512)} %param.13) | copy-start | bytes 6148
  15.1 2.0 %copy-start.6 = (f32[512]{0:T(512)S(1)}, f32[512]{0:T(512)}, u32[]{:S(2)}) copy-start(f32[512]{0:T(512)} %param.14) | copy-start | bytes 6148
  20.1 6.4 %collective-permute-start.1 = (bf16[4,1,512]{2,1,0:T(2,128)(2,1)S(1)}, bf16[4,1,512]{2,1,0:T(2,128)(2,1)S(1)}, u32[]{:S(2)}, u32[]{:S(2)}) collective-permute-start(bf16[4,1,512]{2,1,0:T(2,128)(2,1)S(1)} %slice.49), channel_id=1, source_target_pairs={{1,0},{2,1},{3,2},{5,4},{6,5},{7,6},{9,8},{10,9},{11,10},{13,12},{... | collective-permute-start | bytes 12296 | tf_op jit(solution)/shard_map/ppermute | solution.py:14
  29.6 2.0 %copy-start.3 = (bf16[4,64,512]{2,1,0:T(8,128)(2,1)S(1)}, bf16[4,64,512]{2,1,0:T(8,128)(2,1)}, u32[]{:S(2)}) copy-start(bf16[4,64,512]{2,1,0:T(8,128)(2,1)} %param.17) | copy-start | bytes 786436
  29.6 2.0 %copy-start.4 = (f32[512]{0:T(512)S(1)}, f32[512]{0:T(512)}, u32[]{:S(2)}) copy-start(f32[512]{0:T(512)} %param.15) | copy-start | bytes 6148
  29.6 2.0 %copy-start.7 = (f32[512]{0:T(512)S(1)}, f32[512]{0:T(512)}, u32[]{:S(2)}) copy-start(f32[512]{0:T(512)} %param.16) | copy-start | bytes 6148
  31.3 3.6 %copy-start.2 = (bf16[256,1024]{1,0:T(8,128)(2,1)S(1)}, bf16[256,1024]{1,0:T(8,128)(2,1)}, u32[]{:S(2)}) copy-start(bf16[256,1024]{1,0:T(8,128)(2,1)} %concatenate.27) | copy-start | bytes 1572868
  34.1 0.8 copy-start.1
  37.4 105.9 %all-reduce.3.cloned.1.call-start = ((), (), s32[]{:S(2)}) async-start(), calls=%async_computation.2 | async-start | bytes 1572864 | tf_op jit(solution)/shard_map/psum | solution.py:126
  39.2 10.0 %collective-permute-start.2 = (f32[4,1,512]{2,1,0:T(1,128)S(1)}, f32[4,1,512]{2,1,0:T(1,128)S(1)}, u32[]{:S(2)}, u32[]{:S(2)}) collective-permute-start(f32[4,1,512]{2,1,0:T(1,128)S(1)} %slice.52), channel_id=1, source_target_pairs={{0,1},{1,2},{2,3},{4,5},{5,6},{6,7},{8,9},{9,10},{10,11},{12,13},{... | collective-permute-start | bytes 24584 | tf_op jit(solution)/shard_map/ppermute | solution.py:14
Sparse Core Ops, SparseCore 0:
  37.5 45.6 reduce-scatter.1
  85.5 57.7 all-reduce.2
where the time goes:
time: 153 us; the launch traced here: 152 us
  waiting for transfers between devices  49.6 us (32%)
  blocking collectives  40.2 us (26%)
  other arithmetic  16.1 us (11%)
  local copies, waits for them, and re-layouts  15.2 us (10%)
  between operations  14.3 us (9%)
  matrix products  8.97 us (6%)
  starting transfers between devices  7.65 us (5%)
    psum x1, blocking collectives, on_device(): grad_one_sum, norm_sum = lax.psum((grad_one, norm_terms), ('dp', 'seq'))  40.2 us
    reduce_scatter x1, waiting for transfers between devices, on_device(): lax.psum_scatter(lax.dot_general(patch_two, dpre_two, (((0,), (0,)), ((),...  23.3 us
    psum x1, waiting for transfers between devices, on_device(): grad_two = lax.psum(seq_share, 'dp')  17.9 us
    ppermute x3, waiting for transfers between devices, passed_along(): lax.ppermute(value, axis, [(source, source + steps) for source in range(f...  8.45 us
    ppermute x3, starting transfers between devices, passed_along(): lax.ppermute(value, axis, [(source, source + steps) for source in range(f...  7.57 us
    reshape x1, local copies, waits for them, and re-layouts, on_device(): dpatch_two[:, :, :2 * channels].reshape(clip_count, frames_two, 2, channels)  3.32 us
  transfers between devices with their start and end apart: 5, of which 4 were waited for; matrix products, arithmetic and copies ran while one was open for 14% of the time, Pallas kernels for 0%

commit v1 on v0

--- a/solution.py
+++ b/solution.py
@@ -2,6 +2,7 @@
 import jax.numpy as jnp
 from jax import lax
 from jax.sharding import PartitionSpec as P
+from jax.lax import axis_size, ppermute
 
 epsilon = 1e-05
 root_half = 0.7071067811865476
@@ -123,7 +124,20 @@
         scatter_dimension=0,
         tiled=True,
     )
-    grad_two = lax.psum(seq_share, "dp")
+
+    def limits_point(xs):
+        bus_axis = "dp"
+        chips = axis_size(bus_axis)
+        b_next = xs
+        for t in [
+            [(dev_j, dev_j ^ to_i) for dev_j in range(chips)]
+            for to_i in (1, 2, 4, 8, 16)
+            if to_i < chips
+        ]:
+            b_next = b_next + ppermute(b_next, bus_axis, t)
+        return b_next
+
+    grad_two = limits_point(seq_share)
     return (features, grad_one_sum, grad_two, norm_sum)
 
 

time: 153 us -> 179 us (1.17)
  blocking collectives: 40.2 us -> 55.2 us
  waiting for transfers between devices: 49.6 us -> 55.7 us
  other arithmetic: 16.1 us -> 20 us
  starting transfers between devices: 7.65 us -> 10.1 us
    reduce_scatter x1, waiting for transfers between devices: 23.3 us -> 45.8 us  [on_device(): lax.psum_scatter(lax.dot_general(patch_two, dpre_two, (((0,), (0,)), ((),...]
    psum x1 -> x0, waiting for transfers between devices: 17.9 us -> none  [on_device(): grad_two = lax.psum(seq_share, 'dp')]
    psum x1, blocking collectives: 40.2 us -> 55.2 us  [on_device(): grad_one_sum, norm_sum = lax.psum((grad_one, norm_terms), ('dp', 'seq'))]
    add x0 -> x3, other arithmetic: none -> 4.45 us  [limits_point(): b_next = b_next + ppermute(b_next, bus_axis, t)]
    ppermute x0 -> x3, starting transfers between devices: none -> 3.92 us  [limits_point(): b_next = b_next + ppermute(b_next, bus_axis, t)]
    unnamed x19 -> x20, local copies, waits for them, and re-layouts: 2.9 us -> 0.85 us
    concatenate x2, local copies, waits for them, and re-layouts: 0.57 us -> 2.4 us  [on_device(): jnp.concatenate([passed_along(onward[:, -1:], 'seq', 1), onward[:, :-1]],...]
  transfers between devices with their start and end apart: 5 -> 7, of which waited for: 4 -> 4; matrix products, arithmetic and copies ran while one was open for 14% -> 12% of each run, Pallas kernels for 0% -> 0%
where the time goes in v1:
time: 179 us; the launch traced here: 178 us
  waiting for transfers between devices  55.7 us (31%)
  blocking collectives  55.2 us (31%)
  other arithmetic  20 us (11%)
  local copies, waits for them, and re-layouts  14.9 us (8%)
  between operations  14.3 us (8%)
  starting transfers between devices  10.1 us (6%)
  matrix products  7.84 us (4%)
    psum x1, blocking collectives, on_device(): grad_one_sum, norm_sum = lax.psum((grad_one, norm_terms), ('dp', 'seq'))  55.2 us
    reduce_scatter x1, waiting for transfers between devices, on_device(): lax.psum_scatter(lax.dot_general(patch_two, dpre_two, (((0,), (0,)), ((),...  45.8 us
    ppermute x3, waiting for transfers between devices, passed_along(): lax.ppermute(value, axis, [(source, source + steps) for source in range(f...  8.45 us
    ppermute x3, starting transfers between devices, passed_along(): lax.ppermute(value, axis, [(source, source + steps) for source in range(f...  6.14 us
    add x3, other arithmetic, limits_point(): b_next = b_next + ppermute(b_next, bus_axis, t)  4.45 us
    ppermute x3, starting transfers between devices, limits_point(): b_next = b_next + ppermute(b_next, bus_axis, t)  3.92 us
  transfers between devices with their start and end apart: 7, of which 4 were waited for; matrix products, arithmetic and copies ran while one was open for 12% of the time, Pallas kernels for 0%

profile of v1, /device:TPU:0, one launch (start us, length us, event | category | flops | bytes accessed | tf_op | source)
XLA Modules:
  0.0 178.0 jit_solution(13968397889444541970)
XLA Ops:
  7.2 0.0 copy-start
  7.2 0.0 reduce-scatter.2.cloned.1.call-start
  7.2 0.8 slice.36
  8.0 1.3 collective-permute-start
  9.3 0.7 and_select_fusion
  10.0 4.4 %collective-permute-done = bf16[4,16]{1,0:T(4,128)(2,1)S(1)} collective-permute-done((bf16[4,16]{1,0:T(4,128)(2,1)S(1)}, bf16[4,16]{1,0:T(4,128)(2,1)S(1)}, u32[]{:S(2)}, u32[]{:S(2)}) %collective-permute-start) | collective-permute-done | bytes 160 | tf_op jit(solution)/shard_map/ppermute | solution.py:15
  14.4 0.7 pad_maximum_fusion.6
  15.1 0.0 copy-start.6
  15.1 0.0 copy-start.7
  15.1 0.2 reshape.138
  15.4 0.1 copy.16
  15.5 0.1 copy.17
  15.7 1.1 fusion.49
  16.8 0.3 multiply_reduce_fusion.2
  17.1 0.0 copy-done.6
  17.1 0.0 copy-done.7
  17.1 3.0 %fusion.2 = bf16[512,512]{1,0:T(8,128)(2,1)S(1)} fusion(f32[512,512]{1,0:T(8,128)S(1)} %get-tuple-element.22, f32[512]{0:T(512)S(1)} %copy-done.7, f32[512]{0:T(512)S(1)} %copy-done.6, f32[512]{0:T(512)S(1)} %add_rsqrt_fusion, f32[512]{0:T(512)S(1)} %broadcast_multiply_fusion.2), kind=kLoop, calls=%fused_computation.4 | loop fusion | flops 18087936 | bytes 1581056 | tf_op jit(solution)/shard_map/convert_element_type | solution.py:59
  20.1 1.3 collective-permute-start.1
  21.4 0.1 compare_convert_fusion
  21.5 0.1 reshape.144
  21.6 1.0 concatenate.27
  22.6 4.0 %collective-permute-done.1 = bf16[4,1,512]{2,1,0:T(2,128)(2,1)S(1)} collective-permute-done((bf16[4,1,512]{2,1,0:T(2,128)(2,1)S(1)}, bf16[4,1,512]{2,1,0:T(2,128)(2,1)S(1)}, u32[]{:S(2)}, u32[]{:S(2)}) %collective-permute-start.1) | collective-permute-done | bytes 4128 | tf_op jit(solution)/shard_map/ppermute | solution.py:15
  26.6 0.9 pad_maximum_fusion.2
  27.4 2.1 %slice.41 = bf16[4,64,512]{2,1,0:T(8,128)(2,1)S(1)} slice(bf16[4,129,512]{2,1,0:T(8,128)(2,1)} %pad_maximum_fusion.2), slice={[0:4:1], [2:129:2], [0:512:1]} | slice | bytes 524288 | tf_op jit(solution)/shard_map/slice | solution.py:65
  29.5 0.0 copy-done
  29.6 0.0 copy-start.4
  29.6 0.0 copy-start.5
  29.6 0.0 copy-start.8
  29.6 1.7 fusion.50
  31.3 0.0 copy-start.2
  31.3 0.2 multiply_reduce_fusion.6
  31.6 0.0 copy-done.4
  31.6 0.0 copy-done.5
  31.6 0.0 copy-done.8
  31.6 2.5 %multiply_reduce_fusion.4 = (f32[512]{0:T(512)S(1)}, f32[256]{0:T(256)S(1)}, f32[256]{0:T(256)S(1)}, f32[512]{0:T(512)S(1)}, f32[256,512]{1,0:T(8,128)S(1)}, /*index=5*/bf16[256,512]{1,0:T(8,128)(2,1)}) fusion(f32[256,512]{1,0:T(8,128)S(1)} %get-tuple-element.24, f32[256]{0:T(256)S(1)} %add_rsqrt_fusion.1, f32[256]{0:T(256)S(1)} %broadcast_multiply_fusion.5, ...), kind=kLoop, calls=%fused_computation.54 | loop fusion | flops 11532800 | bytes 1586176 | tf_op jit(solution)/shard_map/reduce_sum | solution.py:114
  34.1 0.0 copy-start.1
  34.1 0.8 copy-done.1
  34.9 0.0 copy-done.2
  34.9 2.4 %fusion.42 = f32[1536,512]{1,0:T(8,128)} fusion(bf16[256,512]{1,0:T(8,128)(2,1)S(1)} %bitcast.40, bf16[256,1024]{1,0:T(8,128)(2,1)S(1)} %copy-done.2, f32[256,512]{1,0:T(8,128)S(1)} %get-tuple-element.15, f32[256,512]{1,0:T(8,128)S(1)} %get-tuple-element.24, f32[256]{0:T(256)S(1)} %get-tuple-element.25, f32[256]{0:T(256)S(1)} %get-tuple-element.26, ...), kind=kOutput, calls=%fused_computation.79 | convolution fusion | flops 405274624 | bytes 4986880 | tf_op jit(solution)/shard_map/dot_general | solution.py:120
  37.3 0.0 reduce-scatter.2.cloned.1.call-update
  37.4 45.8 %reduce-scatter.2.cloned.1.call-done = f32[384,512]{1,0:T(8,128)} async-done(((f32[1536,512]{1,0:T(8,128)}), f32[384,512]{1,0:T(8,128)}) %reduce-scatter.2.cloned.1.call-update) | async-done | bytes 786448 | tf_op jit(solution)/shard_map/reduce_scatter | solution.py:119
  83.1 0.0 collective-permute-start.3
  83.1 1.8 %fusion.51 = f32[256,1536]{1,0:T(8,128)S(1)} fusion(bf16[1536,512]{1,0:T(8,128)(2,1)S(1)} %copy-done, f32[256,512]{1,0:T(8,128)} %copy-done.1, f32[256,512]{1,0:T(8,128)S(1)} %get-tuple-element.24, f32[256]{0:T(256)S(1)} %get-tuple-element.25, f32[256]{0:T(256)S(1)} %get-tuple-element.26, f32[512]{0:T(512)S(1)} %copy-done.5, f32[256]{0:T(256)S(1)} %add_rsqrt_fusion.1, ...), kind=kOutput, calls=%fused_computation.106 | convolution fusion | flops 403701760 | bytes 4200448 | tf_op jit(solution)/shard_map/dot_general | solution.py:92
  85.0 3.6 %collective-permute-start.2 = (f32[4,1,512]{2,1,0:T(1,128)S(1)}, f32[4,1,512]{2,1,0:T(1,128)S(1)}, u32[]{:S(2)}, u32[]{:S(2)}) collective-permute-start(f32[4,1,512]{2,1,0:T(1,128)S(1)} %slice.52), channel_id=1, source_target_pairs={{0,1},{1,2},{2,3},{4,5},{5,6},{6,7},{8,9},{9,10},{10,11},{12,13},{... | collective-permute-start | bytes 24584 | tf_op jit(solution)/shard_map/ppermute | solution.py:15
  88.5 0.0 collective-permute-done.3
  88.5 0.0 copy-done.3
  88.5 0.1 add.112
  88.7 1.5 collective-permute-start.4
  90.2 0.8 slice_bitcast_fusion
  91.1 1.1 slice.50
  92.1 3.1 %reshape.143 = f32[4,64,2,512]{3,2,1,0:T(2,128)} reshape(f32[4,64,1024]{2,1,0:T(8,128)} %slice.50) | data formatting | bytes 2097152 | tf_op jit(solution)/shard_map/reshape | solution.py:95
  95.3 1.6 copy.18
  96.9 0.0 collective-permute-done.2
  96.9 3.0 %slice_add_fusion = (f32[4,64,1,512]{3,2,1,0:T(1,128)S(1)}, f32[4,64,1,512]{3,2,1,0:T(1,128)S(1)}) fusion(f32[4,64,2,512]{3,2,1,0:T(2,128)} %reshape.143, f32[4,63,1,512]{3,2,1,0:T(1,128)S(1)} %copy.18, f32[4,1,1,512]{3,2,1,0:T(1,128)S(1)} %bitcast.45), kind=kLoop, calls=%fused_computation.52 | loop fusion | flops 262144 | bytes 2621440 | tf_op jit(solution)/shard_map/add | solution.py:98
  99.8 1.9 %pad_maximum_fusion = f32[4,64,2,512]{3,2,1,0:T(2,128)} fusion(f32[4,64,1,512]{3,2,1,0:T(1,128)S(1)} %get-tuple-element.17, f32[4,64,1,512]{3,2,1,0:T(1,128)S(1)} %get-tuple-element.16), kind=kLoop, calls=%fused_computation.10 | loop fusion | flops 262144 | bytes 2097152 | tf_op jit(solution)/shard_map/stack | solution.py:98
  101.8 3.0 %reshape_reshape.4 = f32[512,512]{1,0:T(8,128)} reshape(f32[4,64,2,512]{3,2,1,0:T(2,128)} %pad_maximum_fusion) | data formatting | bytes 2097152 | tf_op jit(solution)/shard_map/reshape;reshape | solution.py:101
  104.7 2.3 %multiply_reduce_fusion = (f32[512]{0:T(512)S(1)}, f32[512]{0:T(512)S(1)}, f32[512]{0:T(512)S(1)}, f32[512]{0:T(512)S(1)}, f32[512,512]{1,0:T(8,128)S(1)}) fusion(f32[512,512]{1,0:T(8,128)S(1)} %get-tuple-element.22, f32[512]{0:T(512)S(1)} %add_rsqrt_fusion, f32[512]{0:T(512)S(1)} %broadcast_multiply_fusion.2, f32[512]{0:T(512)S(1)} %copy-done.6, ...), kind=kLoop, calls=%fused_computation.11 | loop fusion | flops 5240832 | bytes 3162112 | tf_op jit(solution)/shard_map/reduce_sum | solution.py:112
  107.0 1.4 collective-permute-done.4
  108.5 2.2 %add.113 = f32[384,512]{1,0:T(8,128)} add(f32[384,512]{1,0:T(8,128)S(1)} %add.112, f32[384,512]{1,0:T(8,128)} %collective-permute-done.4) | non-fusion elementwise | flops 196608 | bytes 2359296 | tf_op jit(solution)/shard_map/add | solution.py:137
  110.6 2.4 %collective-permute-start.5 = (f32[384,512]{1,0:T(8,128)}, f32[384,512]{1,0:T(8,128)S(1)}, u32[]{:S(2)}, u32[]{:S(2)}) collective-permute-start(f32[384,512]{1,0:T(8,128)} %add.113), channel_id=1, source_target_pairs={{0,16},{4,20},{8,24},{12,28},{16,0},{20,4},{24,8},{28,12},{1,17},{... | collective-permute-start | bytes 2359304 | tf_op jit(solution)/shard_map/ppermute | solution.py:137
  113.1 0.8 fusion.8
  113.8 55.2 %all-reduce = (f32[10,512]{1,0:T(8,128)}, f32[4,512]{1,0:T(4,128)}) all-reduce(f32[10,512]{1,0:T(8,128)S(1)} %fusion.8, f32[4,512]{1,0:T(4,128)S(1)} %pad_maximum_fusion.5), channel_id=1, replica_groups=mesh['dp'=8,'seq'=4] {'dp','seq'}, use_global_device_ids=true, to_apply=%region_8.9 | all-reduce | flops 7168 | bytes 57344 | tf_op jit(solution)/shard_map/psum | solution.py:118
  169.0 0.0 collective-permute-done.5
  169.0 2.2 %add.114 = f32[384,512]{1,0:T(8,128)} add(f32[384,512]{1,0:T(8,128)} %add.113, f32[384,512]{1,0:T(8,128)S(1)} %collective-permute-done.5) | non-fusion elementwise | flops 196608 | bytes 2359296 | tf_op jit(solution)/shard_map/add | solution.py:137
  (16 shorter events, 0.2 us)
Async XLA Ops:
  7.2 22.4 %copy-start = (bf16[1536,512]{1,0:T(8,128)(2,1)S(1)}, bf16[1536,512]{1,0:T(8,128)(2,1)}, u32[]{:S(2)}) copy-start(bf16[1536,512]{1,0:T(8,128)(2,1)} %param.12) | copy-start | bytes 4718596
  7.2 76.0 %reduce-scatter.2.cloned.1.call-start = ((), (), s32[]{:S(2)}) async-start(), calls=%async_computation.1 | async-start | bytes 3932160 | tf_op jit(solution)/shard_map/reduce_scatter | solution.py:119
  8.0 6.4 %collective-permute-start = (bf16[4,16]{1,0:T(4,128)(2,1)S(1)}, bf16[4,16]{1,0:T(4,128)(2,1)S(1)}, u32[]{:S(2)}, u32[]{:S(2)}) collective-permute-start(bf16[4,16]{1,0:T(4,128)(2,1)S(1)} %slice.36), channel_id=1, source_target_pairs={{1,0},{2,1},{3,2},{5,4},{6,5},{7,6},{9,8},{10,9},{11,10},{13,12},{... | collective-permute-start | bytes 392 | tf_op jit(solution)/shard_map/ppermute | solution.py:15
  15.1 2.0 %copy-start.6 = (f32[512]{0:T(512)S(1)}, f32[512]{0:T(512)}, u32[]{:S(2)}) copy-start(f32[512]{0:T(512)} %param.13) | copy-start | bytes 6148
  15.1 2.0 %copy-start.7 = (f32[512]{0:T(512)S(1)}, f32[512]{0:T(512)}, u32[]{:S(2)}) copy-start(f32[512]{0:T(512)} %param.14) | copy-start | bytes 6148
  20.1 6.4 %collective-permute-start.1 = (bf16[4,1,512]{2,1,0:T(2,128)(2,1)S(1)}, bf16[4,1,512]{2,1,0:T(2,128)(2,1)S(1)}, u32[]{:S(2)}, u32[]{:S(2)}) collective-permute-start(bf16[4,1,512]{2,1,0:T(2,128)(2,1)S(1)} %slice.49), channel_id=1, source_target_pairs={{1,0},{2,1},{3,2},{5,4},{6,5},{7,6},{9,8},{10,9},{11,10},{13,12},{... | collective-permute-start | bytes 12296 | tf_op jit(solution)/shard_map/ppermute | solution.py:15
  29.6 2.0 %copy-start.4 = (bf16[4,64,512]{2,1,0:T(8,128)(2,1)S(1)}, bf16[4,64,512]{2,1,0:T(8,128)(2,1)}, u32[]{:S(2)}) copy-start(bf16[4,64,512]{2,1,0:T(8,128)(2,1)} %param.17) | copy-start | bytes 786436
  29.6 2.0 %copy-start.5 = (f32[512]{0:T(512)S(1)}, f32[512]{0:T(512)}, u32[]{:S(2)}) copy-start(f32[512]{0:T(512)} %param.15) | copy-start | bytes 6148
  29.6 2.0 %copy-start.8 = (f32[512]{0:T(512)S(1)}, f32[512]{0:T(512)}, u32[]{:S(2)}) copy-start(f32[512]{0:T(512)} %param.16) | copy-start | bytes 6148
  31.3 3.6 %copy-start.2 = (bf16[256,1024]{1,0:T(8,128)(2,1)S(1)}, bf16[256,1024]{1,0:T(8,128)(2,1)}, u32[]{:S(2)}) copy-start(bf16[256,1024]{1,0:T(8,128)(2,1)} %concatenate.27) | copy-start | bytes 1572868
  34.1 0.8 copy-start.1
  83.1 5.4 %copy-start.3 = (f32[384,512]{1,0:T(8,128)S(1)}, f32[384,512]{1,0:T(8,128)}, u32[]{:S(2)}) copy-start(f32[384,512]{1,0:T(8,128)} %reduce-scatter.2.cloned.1.call-done) | copy-start | bytes 2359300
  83.1 5.4 %collective-permute-start.3 = (f32[384,512]{1,0:T(8,128)}, f32[384,512]{1,0:T(8,128)S(1)}, u32[]{:S(2)}, u32[]{:S(2)}) collective-permute-start(f32[384,512]{1,0:T(8,128)} %reduce-scatter.2.cloned.1.call-done), channel_id=1, source_target_pairs={{0,4},{4,0},{8,12},{12,8},{16,20},{20,16},{24,28},{28,24},{1,5},{5... | collective-permute-start | bytes 2359304 | tf_op jit(solution)/shard_map/ppermute | solution.py:137
  85.0 11.9 %collective-permute-start.2 = (f32[4,1,512]{2,1,0:T(1,128)S(1)}, f32[4,1,512]{2,1,0:T(1,128)S(1)}, u32[]{:S(2)}, u32[]{:S(2)}) collective-permute-start(f32[4,1,512]{2,1,0:T(1,128)S(1)} %slice.52), channel_id=1, source_target_pairs={{0,1},{1,2},{2,3},{4,5},{5,6},{6,7},{8,9},{9,10},{10,11},{12,13},{... | collective-permute-start | bytes 24584 | tf_op jit(solution)/shard_map/ppermute | solution.py:15
  88.7 19.8 %collective-permute-start.4 = (f32[384,512]{1,0:T(8,128)S(1)}, f32[384,512]{1,0:T(8,128)}, u32[]{:S(2)}, u32[]{:S(2)}) collective-permute-start(f32[384,512]{1,0:T(8,128)S(1)} %add.112), channel_id=1, source_target_pairs={{0,8},{4,12},{8,0},{12,4},{16,24},{20,28},{24,16},{28,20},{1,9},{5... | collective-permute-start | bytes 2359304 | tf_op jit(solution)/shard_map/ppermute | solution.py:137
  110.6 58.4 %collective-permute-start.5 = (f32[384,512]{1,0:T(8,128)}, f32[384,512]{1,0:T(8,128)S(1)}, u32[]{:S(2)}, u32[]{:S(2)}) collective-permute-start(f32[384,512]{1,0:T(8,128)} %add.113), channel_id=1, source_target_pairs={{0,16},{4,20},{8,24},{12,28},{16,0},{20,4},{24,8},{28,12},{1,17},{... | collective-permute-start | bytes 2359304 | tf_op jit(solution)/shard_map/ppermute | solution.py:137
Sparse Core Ops, SparseCore 0:
  37.5 45.6 reduce-scatter.1
